TPU v7x, 256 devices: a whole 4x4x8 slice. The times are simulated.
256 devices in a mesh: dp: 4 (over y), ctx: 4 (over x), exp: 16 (over z, core).
Axes of the slice: x: 4, y: 4, z: 8, core: 2. Of those that a mesh axis runs over, the one named last changes fastest.
Arguments:
- residual: bfloat16 [4, 768, 4096], P('dp', 'ctx', 'exp'), may hold values from -80 to 80
- ssm_input: bfloat16 [4, 768, 4096], P('dp', 'ctx', 'exp'), may hold values from -80 to 80
- ssm_gate: bfloat16 [4, 768, 4096], P('dp', 'ctx', 'exp'), may hold values from -6 to 6
- input_map: bfloat16 [4, 768, 128], P('dp', 'ctx'), may hold values from -2 to 2
- output_map: bfloat16 [4, 768, 128], P('dp', 'ctx'), may hold values from -2 to 2
- step_raw: float32 [4, 768, 64], P('dp', 'ctx', 'exp'), may hold values from -2 to 2304
- log_rate: float32 [64], P('exp'), may hold values from -12 to 2
- skip_gain: float32 [64], P('exp'), may hold values from 0.5 to 1.5
- head_gain: float32 [4096], P('exp'), may hold values from 0.1 to 1.9
- moe_gain: float32 [4096], replicated, may hold values from 0.1 to 1.9
- expert_ids: int32 [4, 768, 2], P('dp', 'ctx'), may hold values from 0 to 15, all different within a row; in each aligned block of 12 rows (0 to 11, 12 to 23, ..., all dimensions but the last counted through in order) at most 4 rows name the same one
- gate_weight: float32 [4, 768, 2], P('dp', 'ctx'), may hold values from 0.1 to 1
- expert_up: bfloat16 [16, 4096, 12288], P('exp', None, ('dp', 'ctx')), may hold values from -0.09375 to 0.09375
- expert_down: bfloat16 [16, 12288, 4096], P('exp', ('dp', 'ctx')), may hold values from -0.0546875 to 0.0546875
Outputs:
- hidden: bfloat16 [4, 768, 4096], P('dp', 'ctx', 'exp')
- moe_out: bfloat16 [4, 768, 4096], P('dp', ('ctx', 'exp'))
Inputs may be any that keep to these rules, and one draw needn't show every extreme that they name: `expert_ids`: within each aligned block of 12 positions of one sequence, no expert is named by more than 4 routes; some expert is named by exactly 4 routes in some block; the two routes of a position name different experts.
All inputs are finite; a program needn't handle non-finite values.
Results may differ from a plain program's by a relative error of at most 0.02.
Values may be sent and summed in bfloat16 or wider, within the bound.
A program may use at most 64 MiB of HBM per device.

v0:
```python
import jax
import jax.numpy as jnp
from jax import lax
from jax.sharding import PartitionSpec as P

EPSILON = 1e-05


def shifted(block, axis, distance):
    devices = range(lax.axis_size(axis))
    route = [(i - distance, i) for i in devices if i - distance in devices]
    return lax.ppermute(block, axis, route)


def route_slots(routes, experts):
    blocks = routes.shape[0]
    ordered = routes.reshape(blocks, -1)
    matches = (ordered[:, :, None] == jnp.arange(experts, dtype=jnp.int32)[None, None, :]).astype(
        jnp.int32
    )
    earlier = jnp.cumsum(matches, axis=1) - matches
    return jnp.sum(earlier * matches, axis=2).reshape(routes.shape)


def body(
    residual,
    ssm_input,
    ssm_gate,
    input_map,
    output_map,
    step_raw,
    log_rate,
    skip_gain,
    head_gain,
    moe_gain,
    expert_ids,
    gate_weight,
    expert_up,
    expert_down,
):
    heads_loc = log_rate.shape[0]
    local_rows = residual.shape[1]
    width_loc = residual.shape[2]
    head_size = width_loc // heads_loc
    values = ssm_input[0].astype(jnp.float32).reshape(local_rows, heads_loc, head_size)
    step_size = jax.nn.softplus(step_raw[0])
    cumulative = jnp.cumsum(step_size * (-jnp.exp(log_rate))[None, :], axis=0)
    scores = jnp.einsum(
        "tn,sn->ts", output_map[0], input_map[0], preferred_element_type=jnp.float32
    )
    positions = jnp.arange(local_rows)
    causal = positions[:, None] >= positions[None, :]
    spread = cumulative[:, None, :] - cumulative[None, :, :]
    kernel = (
        jnp.where(causal[:, :, None], jnp.exp(jnp.minimum(spread, 0.0)), 0.0)
        * scores[:, :, None]
        * step_size[None, :, :]
    )
    within = jnp.einsum("tsh,shp->thp", kernel, values, precision=lax.Precision.HIGHEST)
    ending = cumulative[-1]
    carried = jnp.exp(ending[None, :] - cumulative) * step_size
    in_map_wide = input_map[0].astype(jnp.float32)
    out_map_wide = output_map[0].astype(jnp.float32)
    local_state = jnp.einsum(
        "sh,shp,sn->hpn", carried, values, in_map_wide, precision=lax.Precision.HIGHEST
    )
    total_decay = jnp.exp(ending)
    incoming = jnp.zeros_like(local_state)
    for repeat in range(lax.axis_size("ctx") - 1):
        outgoing = total_decay[:, None, None] * incoming + local_state
        incoming = shifted(outgoing.astype(jnp.bfloat16), "ctx", 1).astype(outgoing.dtype)
    across_heads = (
        jnp.einsum("tn,hpn->thp", out_map_wide, incoming, precision=lax.Precision.HIGHEST)
        * jnp.exp(cumulative)[:, :, None]
    )
    mixed_y = within + across_heads + skip_gain[None, :, None] * values
    gated = mixed_y * jax.nn.silu(
        ssm_gate[0].astype(jnp.float32).reshape(local_rows, heads_loc, head_size)
    )
    normed = (
        gated
        * lax.rsqrt(jnp.mean(gated * gated, axis=2, keepdims=True) + EPSILON)
        * head_gain.reshape(heads_loc, head_size)
    )
    hidden = (residual[0].astype(jnp.float32) + normed.reshape(local_rows, width_loc)).astype(
        jnp.bfloat16
    )
    exp_count = lax.axis_size("exp")
    my_expert = lax.axis_index("exp")
    tok_rows = local_rows // exp_count
    capacity = min(tok_rows, max(4, 4 * tok_rows // exp_count))
    model_width = width_loc * exp_count
    routes_all = expert_ids[0].reshape(exp_count, tok_rows, 2)
    slots_all = route_slots(routes_all, exp_count)
    targets_all = routes_all * capacity + slots_all
    slot_ids = jnp.arange(exp_count * capacity, dtype=jnp.int32)
    own_targets = lax.dynamic_slice_in_dim(targets_all, my_expert, 1, 0)[0]
    own_weights = lax.dynamic_slice_in_dim(
        gate_weight[0].reshape(exp_count, tok_rows, 2), my_expert, 1, 0
    )[0]
    tokens = lax.all_to_all(hidden, "exp", split_axis=0, concat_axis=1, tiled=True)
    tokens_wide = tokens.astype(jnp.float32)
    normal_rows = (
        tokens_wide
        * lax.rsqrt(jnp.mean(tokens_wide * tokens_wide, axis=1, keepdims=True) + EPSILON)
        * moe_gain[None, :]
    ).astype(jnp.bfloat16)
    placing = jnp.any(slot_ids[:, None, None] == own_targets[None, :, :], axis=2).astype(
        jnp.bfloat16
    )
    outbound = jnp.dot(placing, normal_rows, preferred_element_type=jnp.float32).astype(
        jnp.bfloat16
    )
    outbound = outbound.reshape(exp_count, capacity, model_width)
    arrived = lax.all_to_all(outbound, "exp", split_axis=0, concat_axis=0, tiled=True).reshape(
        exp_count * capacity, model_width
    )
    up_local = expert_up[0]
    down_local = expert_down[0]
    activated = jax.nn.silu(
        jnp.dot(
            lax.all_gather(arrived, ("dp", "ctx"), axis=0, tiled=True),
            up_local,
            preferred_element_type=jnp.float32,
        )
    ).astype(jnp.bfloat16)
    summed = lax.psum_scatter(
        jnp.dot(activated, down_local, preferred_element_type=jnp.float32).astype(jnp.bfloat16),
        ("dp", "ctx"),
        scatter_dimension=0,
        tiled=True,
    )
    sent_back = summed.reshape(exp_count, capacity, model_width)
    returned = lax.all_to_all(sent_back, "exp", split_axis=0, concat_axis=0, tiled=True).reshape(
        exp_count * capacity, model_width
    )
    picking = (own_targets.reshape(-1)[:, None] == slot_ids[None, :]).astype(jnp.bfloat16)
    chosen = jnp.dot(picking, returned, preferred_element_type=jnp.float32).reshape(
        tok_rows, 2, model_width
    )
    combined = jnp.sum(own_weights[:, :, None] * chosen, axis=1).astype(jnp.bfloat16)
    return (hidden[None], combined[None])


def solution(mesh):
    placed = (
        P("dp", "ctx", "exp"),
        P("dp", "ctx", "exp"),
        P("dp", "ctx", "exp"),
        P("dp", "ctx", None),
        P("dp", "ctx", None),
        P("dp", "ctx", "exp"),
        P("exp"),
        P("exp"),
        P("exp"),
        P(),
        P("dp", "ctx", None),
        P("dp", "ctx", None),
        P("exp", None, ("dp", "ctx")),
        P("exp", ("dp", "ctx"), None),
    )
    return jax.shard_map(
        body,
        mesh=mesh,
        in_specs=placed,
        out_specs=(P("dp", "ctx", "exp"), P("dp", ("ctx", "exp"), None)),
        check_vma=False,
    )
```

profile of v0, /device:TPU:33, one launch (start us, length us, event | category | flops | bytes accessed | tf_op | source)
XLA Modules:
  0.0 293.1 jit_solution(14403245142057852232)
XLA Ops:
  7.2 0.7 exponential_negate_fusion
  7.9 0.8 multiply_bitcast_fusion
  8.6 1.2 reduce-window.6
  10.5 0.8 slice_exponential_fusion
  11.2 1.0 copy.38
  12.5 3.1 %collective-permute-start = (bf16[4,64,128]{2,1,0:T(8,128)(2,1)S(1)}, bf16[4,64,128]{2,1,0:T(8,128)(2,1)S(1)}, u32[]{:S(2)}, u32[]{:S(2)}) collective-permute-start(bf16[4,64,128]{2,1,0:T(8,128)(2,1)S(1)} %get-tuple-element.7), channel_id=1, source_target_pairs={{0,16},{16,32},{32,48},{1,17},{17,33},{33,49},{2,18},{18,34},{34,5... | collective-permute-start | bytes 196616 | tf_op jit(solution)/shard_map/ppermute | solution.py:12
  15.6 0.7 fusion.39
  16.4 1.0 fusion.32
  17.4 0.8 copy.41
  18.3 0.8 convolution_bitcast_fusion
  19.2 0.7 fusion.46
  20.0 3.1 %collective-permute-start.1 = (bf16[4,64,128]{2,1,0:T(8,128)(2,1)S(1)}, bf16[4,64,128]{2,1,0:T(8,128)(2,1)S(1)}, u32[]{:S(2)}, u32[]{:S(2)}) collective-permute-start(bf16[4,64,128]{2,1,0:T(8,128)(2,1)S(1)} %add_convert_fusion.3), channel_id=1, source_target_pairs={{0,16},{16,32},{32,48},{1,17},{17,33},{33,49},{2,18},{18,34},{34,5... | collective-permute-start | bytes 196616 | tf_op jit(solution)/shard_map/ppermute | solution.py:12
  23.1 0.7 broadcast_multiply_fusion
  23.8 1.0 copy.39
  24.8 0.8 mul.165
  25.6 2.8 collective-permute-start.2
  28.7 0.9 reshape.142
  29.8 1.1 multiply_reduce_fusion
  31.4 0.7 add_convert_fusion
  32.1 10.9 %all-to-all-start = ((bf16[16,12,256]{2,1,0:T(8,128)(2,1)}), bf16[16,12,256]{2,1,0:T(8,128)(2,1)S(1)}, u32[]{:S(2)}, u32[]{:S(2)}) async-start(bf16[16,12,256]{2,1,0:T(8,128)(2,1)} %add_convert_fusion), calls=%async_computation | async-start | bytes 262144 | tf_op jit(solution)/shard_map/all_to_all | solution.py:101
  43.1 7.7 %all-to-all-done = bf16[16,12,256]{2,1,0:T(8,128)(2,1)S(1)} async-done(((bf16[16,12,256]{2,1,0:T(8,128)(2,1)}), bf16[16,12,256]{2,1,0:T(8,128)(2,1)S(1)}, u32[]{:S(2)}, u32[]{:S(2)}) %all-to-all-start) | async-done | bytes 98336 | tf_op jit(solution)/shard_map/all_to_all | solution.py:101
  51.9 18.3 %all_to_all.20 = bf16[16,4,4096]{2,1,0:T(4,128)(2,1)S(1)} all-to-all(bf16[16,4,4096]{2,1,0:T(4,128)(2,1)S(1)} %reshape.137), channel_id=1, replica_groups=mesh['dp'=4,'ctx'=4,'exp'=16] {'exp'}, dimensions={0} | all-to-all | bytes 1048576 | tf_op jit(solution)/shard_map/all_to_all | solution.py:115
  70.2 1.0 reshape.138
  71.2 75.7 %all-gather.2.cloned.1.call-done = bf16[1024,4096]{1,0:T(8,128)(2,1)} async-done(((bf16[64,4096]{1,0:T(8,128)(2,1)}), bf16[1024,4096]{1,0:T(8,128)(2,1)}) %all-gather.2.cloned.1.call-update) | async-done | bytes 8388624 | tf_op jit(solution)/shard_map/all_gather | solution.py:122
  146.9 11.2 %multiply_convert_fusion = bf16[1024,768]{1,0:T(8,128)(2,1)S(1)} fusion(bf16[1024,4096]{1,0:T(8,128)(2,1)} %all-gather.2.cloned.1.call-done, bf16[1,4096,768]{2,1,0:T(8,128)(2,1)} %param.26), kind=kOutput, calls=%fused_computation.6 | convolution fusion | flops 6446383104 | bytes 16252928 | tf_op jit(solution)/shard_map/dot_general | solution.py:121
  158.1 11.7 %convolution_convert_fusion = bf16[1024,4096]{1,0:T(8,128)(2,1)} fusion(bf16[1024,768]{1,0:T(8,128)(2,1)S(1)} %multiply_convert_fusion, bf16[1,768,4096]{2,1,0:T(8,128)(2,1)} %param.27), kind=kOutput, calls=%fused_computation | convolution fusion | flops 6446645248 | bytes 16252928 | tf_op jit(solution)/shard_map/dot_general | solution.py:128
  169.8 89.5 %reduce-scatter.2.cloned.1.call-done = bf16[64,4096]{1,0:T(8,128)(2,1)} async-done(((bf16[1024,4096]{1,0:T(8,128)(2,1)}), bf16[64,4096]{1,0:T(8,128)(2,1)}) %reduce-scatter.2.cloned.1.call-update) | async-done | bytes 524304 | tf_op jit(solution)/shard_map/reduce_scatter | solution.py:127
  259.4 2.0 reshape.139
  261.4 9.3 %all-to-all-start.2 = ((bf16[16,4,4096]{2,1,0:T(4,128)(2,1)}), bf16[16,4,4096]{2,1,0:T(4,128)(2,1)S(1)}, u32[]{:S(2)}, u32[]{:S(2)}) async-start(bf16[16,4,4096]{2,1,0:T(4,128)(2,1)} %reshape.139), calls=%async_computation.3 | async-start | bytes 1048576 | tf_op jit(solution)/shard_map/all_to_all | solution.py:134
  270.9 0.7 add_convert_fusion.1
  271.6 13.7 %all-to-all-done.2 = bf16[16,4,4096]{2,1,0:T(4,128)(2,1)S(1)} async-done(((bf16[16,4,4096]{2,1,0:T(4,128)(2,1)}), bf16[16,4,4096]{2,1,0:T(4,128)(2,1)S(1)}, u32[]{:S(2)}, u32[]{:S(2)}) %all-to-all-start.2) | async-done | bytes 524320 | tf_op jit(solution)/shard_map/all_to_all | solution.py:134
  285.3 0.9 fusion.5
  (53 shorter events, 3.7 us)
Async XLA Ops:
  7.2 5.1 %copy-start = (bf16[1,192,128]{2,1,0:T(8,128)(2,1)S(1)}, bf16[1,192,128]{2,1,0:T(8,128)(2,1)}, u32[]{:S(2)}) copy-start(bf16[1,192,128]{2,1,0:T(8,128)(2,1)} %param.17) | copy-start | bytes 147460
  7.2 44.1 %copy-start.2 = (f32[4096]{0:T(1024)S(1)}, f32[4096]{0:T(1024)}, u32[]{:S(2)}) copy-start(f32[4096]{0:T(1024)} %param.23) | copy-start | bytes 49156
  12.5 7.3 %collective-permute-start = (bf16[4,64,128]{2,1,0:T(8,128)(2,1)S(1)}, bf16[4,64,128]{2,1,0:T(8,128)(2,1)S(1)}, u32[]{:S(2)}, u32[]{:S(2)}) collective-permute-start(bf16[4,64,128]{2,1,0:T(8,128)(2,1)S(1)} %get-tuple-element.7), channel_id=1, source_target_pairs={{0,16},{16,32},{32,48},{1,17},{17,33},{33,49},{2,18},{18,34},{34,5... | collective-permute-start | bytes 196616 | tf_op jit(solution)/shard_map/ppermute | solution.py:12
  20.0 5.6 %collective-permute-start.1 = (bf16[4,64,128]{2,1,0:T(8,128)(2,1)S(1)}, bf16[4,64,128]{2,1,0:T(8,128)(2,1)S(1)}, u32[]{:S(2)}, u32[]{:S(2)}) collective-permute-start(bf16[4,64,128]{2,1,0:T(8,128)(2,1)S(1)} %add_convert_fusion.3), channel_id=1, source_target_pairs={{0,16},{16,32},{32,48},{1,17},{17,33},{33,49},{2,18},{18,34},{34,5... | collective-permute-start | bytes 196616 | tf_op jit(solution)/shard_map/ppermute | solution.py:12
  25.6 4.1 %collective-permute-start.2 = (bf16[4,64,128]{2,1,0:T(8,128)(2,1)S(1)}, bf16[4,64,128]{2,1,0:T(8,128)(2,1)S(1)}, u32[]{:S(2)}, u32[]{:S(2)}) collective-permute-start(bf16[4,64,128]{2,1,0:T(8,128)(2,1)S(1)} %add_convert_fusion.2), channel_id=1, source_target_pairs={{0,16},{16,32},{32,48},{1,17},{17,33},{33,49},{2,18},{18,34},{34,5... | collective-permute-start | bytes 196616 | tf_op jit(solution)/shard_map/ppermute | solution.py:12
  32.1 18.7 %all-to-all-start = ((bf16[16,12,256]{2,1,0:T(8,128)(2,1)}), bf16[16,12,256]{2,1,0:T(8,128)(2,1)S(1)}, u32[]{:S(2)}, u32[]{:S(2)}) async-start(bf16[16,12,256]{2,1,0:T(8,128)(2,1)} %add_convert_fusion), calls=%async_computation | async-start | bytes 262144 | tf_op jit(solution)/shard_map/all_to_all | solution.py:101
  43.0 103.9 %all-gather.2.cloned.1.call-start = ((), (), s32[]{:S(2)}) async-start(), calls=%async_computation.4 | async-start | bytes 8912896 | tf_op jit(solution)/shard_map/all_gather | solution.py:122
  71.1 188.2 %reduce-scatter.2.cloned.1.call-start = ((), (), s32[]{:S(2)}) async-start(), calls=%async_computation.5 | async-start | bytes 8912896 | tf_op jit(solution)/shard_map/reduce_scatter | solution.py:127
  169.8 100.8 %copy-start.3 = (f32[1,192,2]{1,2,0:T(2,128)S(1)}, f32[1,192,2]{1,2,0:T(2,128)}, u32[]{:S(2)}) copy-start(f32[1,192,2]{1,2,0:T(2,128)} %param.25) | copy-start | bytes 4612
  169.8 101.1 %copy-start.1 = (bf16[1,192,256]{2,1,0:T(8,128)(2,1)S(1)}, bf16[1,192,256]{2,1,0:T(8,128)(2,1)}, u32[]{:S(2)}) copy-start(bf16[1,192,256]{2,1,0:T(8,128)(2,1)} %param.14) | copy-start | bytes 294916
  261.4 23.8 %all-to-all-start.2 = ((bf16[16,4,4096]{2,1,0:T(4,128)(2,1)}), bf16[16,4,4096]{2,1,0:T(4,128)(2,1)S(1)}, u32[]{:S(2)}, u32[]{:S(2)}) async-start(bf16[16,4,4096]{2,1,0:T(4,128)(2,1)} %reshape.139), calls=%async_computation.3 | async-start | bytes 1048576 | tf_op jit(solution)/shard_map/all_to_all | solution.py:134
Sparse Core Ops, SparseCore 0:
  71.3 75.6 all-gather.1
  170.0 89.3 reduce-scatter.1
where the time goes:
time: 298 us; the launch traced here: 293 us
  waiting for transfers between devices  187 us (63%)
  starting transfers between devices  29.3 us (10%)
  matrix products  27.3 us (9%)
  blocking collectives  18.3 us (6%)
  between operations  14.3 us (5%)
  local copies, waits for them, and re-layouts  9.67 us (3%)
  other arithmetic  7.5 us (3%)
    reduce_scatter x1, waiting for transfers between devices, body(): lax.psum_scatter(jnp.dot(activated, down_local, preferred_element_type=jn...  89.5 us
    all_gather x1, waiting for transfers between devices, body(): lax.all_gather(arrived, ('dp', 'ctx'), axis=0, tiled=True)  75.7 us
    all_to_all x1, blocking collectives, body(): lax.all_to_all(outbound, 'exp', split_axis=0, concat_axis=0, tiled=True)  18.3 us
    all_to_all x1, waiting for transfers between devices, body(): lax.all_to_all(sent_back, 'exp', split_axis=0, concat_axis=0, tiled=True)  13.7 us
    dot_general x1, matrix products, body(): jnp.dot(activated, down_local, preferred_element_type=jnp.float32)  11.7 us
    dot_general x1, matrix products, body(): jnp.dot(lax.all_gather(arrived, ('dp', 'ctx'), axis=0, tiled=True), up_lo...  11.2 us
    all_to_all x1, starting transfers between devices, body(): lax.all_to_all(hidden, 'exp', split_axis=0, concat_axis=1, tiled=True)  10.9 us
    all_to_all x1, starting transfers between devices, body(): lax.all_to_all(sent_back, 'exp', split_axis=0, concat_axis=0, tiled=True)  9.25 us
  transfers between devices with their start and end apart: 7, of which 5 were waited for; matrix products, arithmetic and copies ran while one was open for 3% of the time, Pallas kernels for 0%

commit v1 on v0

--- a/solution.py
+++ b/solution.py
@@ -1,6 +1,8 @@
 import jax
 import jax.numpy as jnp
 from jax import lax
+from jax.experimental import pallas as pl
+from jax.experimental.pallas import tpu as pltpu
 from jax.sharding import PartitionSpec as P
 
 EPSILON = 1e-05
@@ -20,6 +22,219 @@
     )
     earlier = jnp.cumsum(matches, axis=1) - matches
     return jnp.sum(earlier * matches, axis=2).reshape(routes.shape)
+
+
+ROWS = 16
+MESH = pl.DeviceIdType.MESH
+
+
+def plane_kernel(
+    x_ref, up_hbm, down_hbm, out_ref,
+    gath, part, red1, red2, act, up_v, down_v,
+    wsem, ag_send, ag_recv, r1_send, r1_recv, r2_send, r2_recv,
+):
+    dp, ctx, ex = lax.axis_index("dp"), lax.axis_index("ctx"), lax.axis_index("exp")
+    n = 4
+    width = x_ref.shape[1]
+    ffd = up_v.shape[1]
+
+    def rows(p, j):
+        return pl.ds(pl.multiple_of((p * n + j) * ROWS, ROWS), ROWS)
+
+    def target(p, phase):
+        step = 1 - 2 * lax.rem(p, 2)
+        on_ctx = lax.rem(p // 2 + phase, 2)
+        d = lax.rem(dp + n + step * on_ctx, n)
+        c = lax.rem(ctx + n + step * (1 - on_ctx), n)
+        return (d, c, ex)
+
+    def gather(s, p, j):
+        if s == 0:
+            src, phase = gath.at[0, rows(p, j - 1), :], 0
+        else:
+            src, phase = gath.at[s - 1, rows(p, j), :], 1
+        return pltpu.make_async_remote_copy(
+            src_ref=src, dst_ref=gath.at[s, rows(p, j), :],
+            send_sem=ag_send.at[s, p, j], recv_sem=ag_recv.at[s, p, j],
+            device_id=target(p, phase), device_id_type=MESH,
+        )
+
+    def first_gather(s, p, j, phase):
+        return pltpu.make_async_remote_copy(
+            src_ref=x_ref.at[pl.ds(pl.multiple_of(p * ROWS, ROWS), ROWS), :],
+            dst_ref=gath.at[s, rows(p, j), :],
+            send_sem=ag_send.at[s, p, j], recv_sem=ag_recv.at[s, p, j],
+            device_id=target(p, phase), device_id_type=MESH,
+        )
+
+    def reduce1(s, p, j):
+        return pltpu.make_async_remote_copy(
+            src_ref=part.at[s, rows(p, j), :], dst_ref=red1.at[s - 1, rows(p, j), :],
+            send_sem=r1_send.at[s - 1, p, j], recv_sem=r1_recv.at[s - 1, p, j],
+            device_id=target(p, 1), device_id_type=MESH,
+        )
+
+    def reduce2(k, p):
+        return pltpu.make_async_remote_copy(
+            src_ref=part.at[0, rows(p, k), :], dst_ref=red2.at[k - 1, rows(0, p), :],
+            send_sem=r2_send.at[k - 1, p], recv_sem=r2_recv.at[k - 1, p],
+            device_id=target(p, 0), device_id_type=MESH,
+        )
+
+    up_copy = pltpu.make_async_copy(up_hbm, up_v, wsem.at[0])
+    down_copy = pltpu.make_async_copy(down_hbm, down_v, wsem.at[1])
+    up_copy.start()
+    down_copy.start()
+
+    barrier = pltpu.get_barrier_semaphore()
+    for p in (0, 1, 2, 3):
+        pl.semaphore_signal(barrier, inc=1, device_id=target(p, 0), device_id_type=MESH)
+    pl.semaphore_wait(barrier, 4)
+
+    @pl.loop(0, 4)
+    def _(p):
+        first_gather(0, p, 1, 0).start()
+        first_gather(1, p, 0, 1).start()
+
+    @pl.loop(0, 4)
+    def _(p):
+        gath[0, rows(p, 0), :] = x_ref[pl.ds(pl.multiple_of(p * ROWS, ROWS), ROWS), :]
+
+    def forward(s, j):
+        @pl.loop(0, 4)
+        def _(p):
+            gather(s, p, j).wait_recv()
+            if s == 0 and j < 3:
+                gather(0, p, j + 1).start()
+            if s < 3:
+                gather(s + 1, p, j).start()
+
+    def up(s, c):
+        cols = pl.ds(pl.multiple_of(c * 256, 256), 256)
+        h = jnp.dot(gath[s], up_v[:, cols], preferred_element_type=jnp.float32)
+        act[:, cols] = jax.nn.silu(h).astype(jnp.bfloat16)
+
+    def down(s, c):
+        cols = pl.ds(pl.multiple_of(c * 512, 512), 512)
+        part[s, :, cols] = jnp.dot(
+            act[...], down_v[:, cols], preferred_element_type=jnp.float32
+        ).astype(jnp.bfloat16)
+
+    def ups(s):
+        @pl.loop(0, ffd // 256)
+        def _(c):
+            up(s, c)
+
+    def downs(s, lo, hi):
+        @pl.loop(lo, hi)
+        def _(c):
+            down(s, c)
+
+    nd = width // 512
+
+    def add(dst, d_idx, src, s_idx):
+        dst[d_idx] = (
+            dst[d_idx].astype(jnp.float32) + src[s_idx].astype(jnp.float32)
+        ).astype(jnp.bfloat16)
+
+    forward(0, 1)
+    forward(0, 2)
+    forward(1, 0)
+    forward(0, 3)
+    up_copy.wait()
+    down_copy.wait()
+    ups(0)
+    forward(1, 1)
+    downs(0, 0, nd // 2)
+    forward(1, 2)
+    downs(0, nd // 2, nd)
+    forward(1, 3)
+    forward(2, 0)
+    ups(1)
+    forward(2, 1)
+    downs(1, 0, nd // 2)
+    forward(2, 2)
+    downs(1, nd // 2, nd)
+    forward(2, 3)
+    for j in (1, 2, 3, 0):
+        @pl.loop(0, 4)
+        def _(p):
+            reduce1(1, p, j).start()
+    ups(2)
+    downs(2, 0, nd)
+    for j in range(4):
+        forward(3, j)
+    ups(3)
+    downs(3, 0, nd)
+    for s in (2, 3):
+        for j in (1, 2, 3, 0):
+            @pl.loop(0, 4)
+            def _(p):
+                reduce1(s - 1, p, j).wait_recv()
+                add(part, (s, rows(p, j), slice(None)), red1, (s - 2, rows(p, j), slice(None)))
+                reduce1(s, p, j).start()
+    for j in (1, 2, 3, 0):
+        @pl.loop(0, 4)
+        def _(p):
+            reduce1(3, p, j).wait_recv()
+            add(part, (0, rows(p, j), slice(None)), red1, (2, rows(p, j), slice(None)))
+            if j != 1:
+                k = 3 if j == 0 else j - 1
+                reduce2(k, p).wait_recv()
+                add(part, (0, rows(p, j), slice(None)), red2, (k - 1, rows(0, p), slice(None)))
+            if j != 0:
+                reduce2(j, p).start()
+            else:
+                out_ref[pl.ds(pl.multiple_of(p * ROWS, ROWS), ROWS), :] = part[0, rows(p, 0), :]
+
+    @pl.loop(0, 4)
+    def _(p):
+        first_gather(0, p, 1, 0).wait_send()
+        first_gather(1, p, 0, 1).wait_send()
+        for j in (2, 3):
+            gather(0, p, j).wait_send()
+        for s in (1, 2, 3):
+            for j in range(4):
+                if s > 1 or j > 0:
+                    gather(s, p, j).wait_send()
+                reduce1(s, p, j).wait_send()
+            reduce2(s, p).wait_send()
+
+
+def plane_experts(arrived, up_local, down_local):
+    slots, width = arrived.shape
+    ffd = up_local.shape[1]
+    bf = jnp.bfloat16
+    dma = pltpu.SemaphoreType.DMA
+    return pl.pallas_call(
+        plane_kernel,
+        out_shape=jax.ShapeDtypeStruct((slots, width), bf),
+        in_specs=[
+            pl.BlockSpec(memory_space=pltpu.VMEM),
+            pl.BlockSpec(memory_space=pl.ANY),
+            pl.BlockSpec(memory_space=pl.ANY),
+        ],
+        out_specs=pl.BlockSpec(memory_space=pltpu.VMEM),
+        scratch_shapes=[
+            pltpu.VMEM((4, 16 * ROWS, width), bf),
+            pltpu.VMEM((4, 16 * ROWS, width), bf),
+            pltpu.VMEM((3, 16 * ROWS, width), bf),
+            pltpu.VMEM((3, 4 * ROWS, width), bf),
+            pltpu.VMEM((16 * ROWS, ffd), bf),
+            pltpu.VMEM((width, ffd), bf),
+            pltpu.VMEM((ffd, width), bf),
+            dma((2,)),
+            dma((4, 4, 4)),
+            dma((4, 4, 4)),
+            dma((3, 4, 4)),
+            dma((3, 4, 4)),
+            dma((3, 4)),
+            dma((3, 4)),
+        ],
+        compiler_params=pltpu.CompilerParams(
+            collective_id=0, has_side_effects=True, vmem_limit_bytes=56 * 2**20
+        ),
+    )(arrived, up_local, down_local)
 
 
 def body(
@@ -115,21 +330,7 @@
     arrived = lax.all_to_all(outbound, "exp", split_axis=0, concat_axis=0, tiled=True).reshape(
         exp_count * capacity, model_width
     )
-    up_local = expert_up[0]
-    down_local = expert_down[0]
-    activated = jax.nn.silu(
-        jnp.dot(
-            lax.all_gather(arrived, ("dp", "ctx"), axis=0, tiled=True),
-            up_local,
-            preferred_element_type=jnp.float32,
-        )
-    ).astype(jnp.bfloat16)
-    summed = lax.psum_scatter(
-        jnp.dot(activated, down_local, preferred_element_type=jnp.float32).astype(jnp.bfloat16),
-        ("dp", "ctx"),
-        scatter_dimension=0,
-        tiled=True,
-    )
+    summed = plane_experts(arrived, expert_up[0], expert_down[0])
     sent_back = summed.reshape(exp_count, capacity, model_width)
     returned = lax.all_to_all(sent_back, "exp", split_axis=0, concat_axis=0, tiled=True).reshape(
         exp_count * capacity, model_width

time: 298 us -> 192 us (0.64)
  the two profiles are of different devices: /device:TPU:33 before, /device:TPU:1 now
where the time goes in v1:
time: 192 us; the launch traced here: 191 us
  Pallas kernels  98.1 us (51%)
  starting transfers between devices  25.8 us (13%)
  waiting for transfers between devices  25.2 us (13%)
  blocking collectives  19.9 us (10%)
  local copies, waits for them, and re-layouts  9.65 us (5%)
  other arithmetic  7.49 us (4%)
  matrix products  4.44 us (2%)
    pallas_call x1, Pallas kernels, plane_experts(): pl.pallas_call(plane_kernel, out_shape=jax.ShapeDtypeStruct((slots, width...  98.1 us
    all_to_all x1, blocking collectives, body(): lax.all_to_all(outbound, 'exp', split_axis=0, concat_axis=0, tiled=True)  19.9 us
    all_to_all x1, waiting for transfers between devices, body(): lax.all_to_all(sent_back, 'exp', split_axis=0, concat_axis=0, tiled=True)  16.3 us
    all_to_all x1, starting transfers between devices, body(): lax.all_to_all(hidden, 'exp', split_axis=0, concat_axis=1, tiled=True)  11.2 us
    ppermute x3, starting transfers between devices, shifted(): return lax.ppermute(block, axis, route)  9.89 us
    all_to_all x1, waiting for transfers between devices, body(): lax.all_to_all(hidden, 'exp', split_axis=0, concat_axis=1, tiled=True)  8.8 us
    all_to_all x1, starting transfers between devices, body(): lax.all_to_all(sent_back, 'exp', split_axis=0, concat_axis=0, tiled=True)  4.76 us
  transfers between devices with their start and end apart: 5, of which 3 were waited for; matrix products, arithmetic and copies ran while one was open for 5% of the time, Pallas kernels for 0%

profile of v1, /device:TPU:1, one launch (start us, length us, event | category | flops | bytes accessed | tf_op | source)
XLA Modules:
  0.0 191.5 jit_solution(2305479847363017534)
XLA Ops:
  0.7 0.7 exponential_negate_fusion
  1.3 0.8 multiply_bitcast_fusion
  2.1 1.2 reduce-window.6
  3.9 0.8 slice_exponential_fusion
  4.7 1.0 copy.38
  5.7 0.3 add_convert_fusion.4
  6.0 3.9 %collective-permute-start = (bf16[4,64,128]{2,1,0:T(8,128)(2,1)S(1)}, bf16[4,64,128]{2,1,0:T(8,128)(2,1)S(1)}, u32[]{:S(2)}, u32[]{:S(2)}) collective-permute-start(bf16[4,64,128]{2,1,0:T(8,128)(2,1)S(1)} %get-tuple-element.7), channel_id=1, source_target_pairs={{0,16},{16,32},{32,48},{1,17},{17,33},{33,49},{2,18},{18,34},{34,5... | collective-permute-start | bytes 196616 | tf_op jit(solution)/shard_map/ppermute | solution.py:14
  9.9 0.7 fusion.34
  10.7 1.0 fusion.27
  11.7 0.8 copy.41
  12.6 0.8 convolution_bitcast_fusion
  13.5 0.7 fusion.41
  14.2 3.1 %collective-permute-start.1 = (bf16[4,64,128]{2,1,0:T(8,128)(2,1)S(1)}, bf16[4,64,128]{2,1,0:T(8,128)(2,1)S(1)}, u32[]{:S(2)}, u32[]{:S(2)}) collective-permute-start(bf16[4,64,128]{2,1,0:T(8,128)(2,1)S(1)} %add_convert_fusion.3), channel_id=1, source_target_pairs={{0,16},{16,32},{32,48},{1,17},{17,33},{33,49},{2,18},{18,34},{34,5... | collective-permute-start | bytes 196616 | tf_op jit(solution)/shard_map/ppermute | solution.py:14
  17.4 0.7 broadcast_multiply_fusion
  18.0 1.0 copy.39
  19.0 0.8 mul.161
  19.9 2.8 %collective-permute-start.2 = (bf16[4,64,128]{2,1,0:T(8,128)(2,1)S(1)}, bf16[4,64,128]{2,1,0:T(8,128)(2,1)S(1)}, u32[]{:S(2)}, u32[]{:S(2)}) collective-permute-start(bf16[4,64,128]{2,1,0:T(8,128)(2,1)S(1)} %add_convert_fusion.2), channel_id=1, source_target_pairs={{0,16},{16,32},{32,48},{1,17},{17,33},{33,49},{2,18},{18,34},{34,5... | collective-permute-start | bytes 196616 | tf_op jit(solution)/shard_map/ppermute | solution.py:14
  23.0 0.9 reshape.142
  24.0 1.1 multiply_reduce_fusion
  25.4 0.2 reshape.136
  25.7 0.7 add_convert_fusion
  26.4 11.2 %all-to-all-start = ((bf16[16,12,256]{2,1,0:T(8,128)(2,1)}), bf16[16,12,256]{2,1,0:T(8,128)(2,1)S(1)}, u32[]{:S(2)}, u32[]{:S(2)}) async-start(bf16[16,12,256]{2,1,0:T(8,128)(2,1)} %add_convert_fusion), calls=%async_computation | async-start | bytes 262144 | tf_op jit(solution)/shard_map/all_to_all | solution.py:316
  37.6 8.8 %all-to-all-done = bf16[16,12,256]{2,1,0:T(8,128)(2,1)S(1)} async-done(((bf16[16,12,256]{2,1,0:T(8,128)(2,1)}), bf16[16,12,256]{2,1,0:T(8,128)(2,1)S(1)}, u32[]{:S(2)}, u32[]{:S(2)}) %all-to-all-start) | async-done | bytes 98336 | tf_op jit(solution)/shard_map/all_to_all | solution.py:316
  46.9 0.4 convolution_convert_fusion
  47.5 19.9 %all_to_all.20 = bf16[16,4,4096]{2,1,0:T(4,128)(2,1)S(1)} all-to-all(bf16[16,4,4096]{2,1,0:T(4,128)(2,1)S(1)} %reshape.137), channel_id=1, replica_groups=mesh['dp'=4,'ctx'=4,'exp'=16] {'exp'}, dimensions={0} | all-to-all | bytes 1048576 | tf_op jit(solution)/shard_map/all_to_all | solution.py:330
  67.4 0.9 reshape.138.x_ref
  68.3 98.1 %shard_map.149 = bf16[64,4096]{1,0:T(8,128)(2,1)} custom-call(bf16[64,4096]{1,0:T(8,128)(2,1)} %reshape.138.x_ref, bf16[4096,768]{1,0:T(8,128)(2,1)} %bitcast.88, bf16[768,4096]{1,0:T(8,128)(2,1)} %bitcast.89), custom_call_target="tpu_custom_call" | custom-call | tf_op jit(solution)/shard_map/pallas_call | solution.py:209
  166.4 2.0 %reshape.139 = bf16[16,4,4096]{2,1,0:T(4,128)(2,1)} reshape(bf16[64,4096]{1,0:T(8,128)(2,1)} %shard_map.149) | data formatting | bytes 1048576 | tf_op jit(solution)/shard_map/reshape | solution.py:334
  168.4 4.8 %all-to-all-start.2 = ((bf16[16,4,4096]{2,1,0:T(4,128)(2,1)}), bf16[16,4,4096]{2,1,0:T(4,128)(2,1)S(1)}, u32[]{:S(2)}, u32[]{:S(2)}) async-start(bf16[16,4,4096]{2,1,0:T(4,128)(2,1)} %reshape.139), calls=%async_computation.2 | async-start | bytes 1048576 | tf_op jit(solution)/shard_map/all_to_all | solution.py:335
  173.4 0.7 add_convert_fusion.1
  174.1 16.3 %all-to-all-done.2 = bf16[16,4,4096]{2,1,0:T(4,128)(2,1)S(1)} async-done(((bf16[16,4,4096]{2,1,0:T(4,128)(2,1)}), bf16[16,4,4096]{2,1,0:T(4,128)(2,1)S(1)}, u32[]{:S(2)}, u32[]{:S(2)}) %all-to-all-start.2) | async-done | bytes 524320 | tf_op jit(solution)/shard_map/all_to_all | solution.py:335
  190.5 0.9 fusion
  (46 shorter events, 2.8 us)
Async XLA Ops:
  0.6 5.1 %copy-start = (bf16[1,192,128]{2,1,0:T(8,128)(2,1)S(1)}, bf16[1,192,128]{2,1,0:T(8,128)(2,1)}, u32[]{:S(2)}) copy-start(bf16[1,192,128]{2,1,0:T(8,128)(2,1)} %param.17) | copy-start | bytes 147460
  0.6 46.3 %copy-start.2 = (f32[4096]{0:T(1024)S(1)}, f32[4096]{0:T(1024)}, u32[]{:S(2)}) copy-start(f32[4096]{0:T(1024)} %param.23) | copy-start | bytes 49156
  6.0 8.1 %collective-permute-start = (bf16[4,64,128]{2,1,0:T(8,128)(2,1)S(1)}, bf16[4,64,128]{2,1,0:T(8,128)(2,1)S(1)}, u32[]{:S(2)}, u32[]{:S(2)}) collective-permute-start(bf16[4,64,128]{2,1,0:T(8,128)(2,1)S(1)} %get-tuple-element.7), channel_id=1, source_target_pairs={{0,16},{16,32},{32,48},{1,17},{17,33},{33,49},{2,18},{18,34},{34,5... | collective-permute-start | bytes 196616 | tf_op jit(solution)/shard_map/ppermute | solution.py:14
  14.2 5.6 %collective-permute-start.1 = (bf16[4,64,128]{2,1,0:T(8,128)(2,1)S(1)}, bf16[4,64,128]{2,1,0:T(8,128)(2,1)S(1)}, u32[]{:S(2)}, u32[]{:S(2)}) collective-permute-start(bf16[4,64,128]{2,1,0:T(8,128)(2,1)S(1)} %add_convert_fusion.3), channel_id=1, source_target_pairs={{0,16},{16,32},{32,48},{1,17},{17,33},{33,49},{2,18},{18,34},{34,5... | collective-permute-start | bytes 196616 | tf_op jit(solution)/shard_map/ppermute | solution.py:14
  19.9 4.1 %collective-permute-start.2 = (bf16[4,64,128]{2,1,0:T(8,128)(2,1)S(1)}, bf16[4,64,128]{2,1,0:T(8,128)(2,1)S(1)}, u32[]{:S(2)}, u32[]{:S(2)}) collective-permute-start(bf16[4,64,128]{2,1,0:T(8,128)(2,1)S(1)} %add_convert_fusion.2), channel_id=1, source_target_pairs={{0,16},{16,32},{32,48},{1,17},{17,33},{33,49},{2,18},{18,34},{34,5... | collective-permute-start | bytes 196616 | tf_op jit(solution)/shard_map/ppermute | solution.py:14
  26.4 20.0 %all-to-all-start = ((bf16[16,12,256]{2,1,0:T(8,128)(2,1)}), bf16[16,12,256]{2,1,0:T(8,128)(2,1)S(1)}, u32[]{:S(2)}, u32[]{:S(2)}) async-start(bf16[16,12,256]{2,1,0:T(8,128)(2,1)} %add_convert_fusion), calls=%async_computation | async-start | bytes 262144 | tf_op jit(solution)/shard_map/all_to_all | solution.py:316
  68.3 104.9 %copy-start.3 = (f32[1,192,2]{1,2,0:T(2,128)S(1)}, f32[1,192,2]{1,2,0:T(2,128)}, u32[]{:S(2)}) copy-start(f32[1,192,2]{1,2,0:T(2,128)} %param.25) | copy-start | bytes 4612
  68.3 105.1 %copy-start.1 = (bf16[1,192,256]{2,1,0:T(8,128)(2,1)S(1)}, bf16[1,192,256]{2,1,0:T(8,128)(2,1)}, u32[]{:S(2)}) copy-start(bf16[1,192,256]{2,1,0:T(8,128)(2,1)} %param.14) | copy-start | bytes 294916
  168.4 22.0 %all-to-all-start.2 = ((bf16[16,4,4096]{2,1,0:T(4,128)(2,1)}), bf16[16,4,4096]{2,1,0:T(4,128)(2,1)S(1)}, u32[]{:S(2)}, u32[]{:S(2)}) async-start(bf16[16,4,4096]{2,1,0:T(4,128)(2,1)} %reshape.139), calls=%async_computation.2 | async-start | bytes 1048576 | tf_op jit(solution)/shard_map/all_to_all | solution.py:335
